TPU v7x, 32 devices: a whole 2x2x4 slice. The times are simulated.
32 devices in a mesh: patch: 16 (over z, y, core), chan: 2 (over x).
Axes of the slice: x: 2, y: 2, z: 4, core: 2. Of those that a mesh axis runs over, the one named last changes fastest.
Arguments:
- fields: bfloat16 [16, 128, 1024], P('patch', 'chan'), may hold values from -6 to 6
- w_one: bfloat16 [9, 512, 128], P(None, 'chan'), may hold values from -0.1875 to 0.1875
- bias_one: float32 [512], P('chan'), may hold values from -3 to 3
- w_two: bfloat16 [9, 128, 512], P(None, None, 'chan'), may hold values from -0.09375 to 0.09375
- neighbour: int32 [16, 4], replicated, may hold values from 0 to 15, as said below
- seam_code: int32 [16, 4], replicated, may hold values from 0 to 7, as said below
- band_order: int32 [16], replicated, may hold values from 0 to 15, each once
- target: bfloat16 [16, 128, 1024], P('patch', 'chan'), may hold values from -6 to 6
- lat_weight: bfloat16 [16, 1024], P('patch'), may hold values from 0.099609375 to 1
Outputs:
- loss_value: float32 [], replicated
- grad_one: float32 [9, 512, 128], P(None, 'chan')
- grad_two: float32 [9, 128, 512], P(None, None, 'chan')
- grad_bias: float32 [512], P('chan')
Inputs may be any that keep to these rules, and one draw needn't show every extreme that they name: The sides of all patches are paired: side s of patch p borders side t = seam_code[p, s] mod 4 of patch q = neighbour[p, s], and then neighbour[q, t] = p, seam_code[q, t] mod 4 = s, and both codes agree on being 4 or more; so every edge is read by exactly one side of one other patch, and the four sides of a patch face four different patches. `seam_code`: code mod 4 names the neighbour's edge that forms the seam; codes 4 and above run that edge reversed, alike on both sides of a seam. `band_order`: each patch fills exactly one slot of every band.
All inputs are finite; a program needn't handle non-finite values.
Results may differ from a plain program's by a relative error of at most 0.0021.
Values may be sent and summed in bfloat16 or wider, within the bound.
A program may use at most 64 MiB of HBM per device.

v0:
```python
import math
import jax
import jax.numpy as jnp
from jax import lax
from jax.sharding import PartitionSpec as P

P_SIZE = 32


def edges_of(grid):
    return jnp.stack([grid[0], grid[-1], grid[:, 0], grid[:, -1]])


def with_frame(grid, strips):
    rows = jnp.concatenate([strips[0][None], grid, strips[1][None]], axis=0)
    left = jnp.pad(strips[2], ((1, 1), (0, 0)))[:, None]
    right = jnp.pad(strips[3], ((1, 1), (0, 0)))[:, None]
    return jnp.concatenate([left, rows, right], axis=1)


def conv(values, weight, pad, spec):
    return lax.conv_general_dilated(
        values[None],
        weight,
        (1, 1),
        ((pad, pad), (pad, pad)),
        dimension_numbers=("NHWC", spec, "NHWC"),
        preferred_element_type=jnp.float32,
    )[0]


def smooth_gate(values):
    return jax.nn.gelu(values, approximate=True)


def on_device(fields, w_one, bias_one, w_two, neighbour, seam_code, band_order, target, lat_weight):
    length = P_SIZE
    cells = length * length
    count = lax.axis_size("patch")
    chans = lax.axis_size("chan")
    part = cells // count
    own = lax.axis_index("patch")
    own_nbr = lax.dynamic_slice_in_dim(neighbour, own, 1, 0)[0]
    own_code = lax.dynamic_slice_in_dim(seam_code, own, 1, 0)[0]
    ids = jnp.arange(count, dtype=jnp.int32)
    faces = (own_nbr[:, None] == ids[None, :]).astype(jnp.bfloat16)
    turned = (own_code >= 4)[:, None, None]
    inner = w_one.shape[1]

    def to_send(grid):
        strips = edges_of(grid)
        strips = jnp.where(turned, strips[:, ::-1], strips)
        return jnp.einsum("tr,tkc->rkc", faces, strips, preferred_element_type=jnp.float32).astype(
            jnp.bfloat16
        )

    def picked(arrived):
        return jnp.einsum("tr,rkc->tkc", faces, arrived, preferred_element_type=jnp.float32).astype(
            jnp.bfloat16
        )

    def swap(sent):
        return lax.all_to_all(sent, "patch", split_axis=0, concat_axis=0, tiled=True)

    both = lax.all_gather(jnp.stack([fields[0], target[0]]), "chan", axis=1, tiled=True)
    chan_full = both.shape[1]
    x_grid = both[0].T.reshape(length, length, chan_full)
    slots = (band_order[None, :] == ids[:, None]).astype(jnp.bfloat16)
    lat_rows = -(-part // chan_full)
    lat_parts = jnp.pad(
        lat_weight.reshape(count, part), ((0, 0), (0, lat_rows * chan_full - part))
    ).reshape(count, lat_rows, chan_full)
    band_parts = jnp.concatenate([both[1].T.reshape(count, part, chan_full), lat_parts], axis=1)
    band_parts = jnp.einsum(
        "ps,skc->pkc", slots, band_parts, preferred_element_type=jnp.float32
    ).astype(jnp.bfloat16)
    first = swap(jnp.concatenate([to_send(x_grid), band_parts], axis=1))
    x_pad = with_frame(x_grid, picked(first[:, :length]))
    target_patch = first[:, length : length + part].reshape(cells, chan_full)
    lat_w = (
        first[:, length + part :]
        .reshape(count, lat_rows * chan_full)[:, :part]
        .reshape(cells, 1)
        .astype(jnp.float32)
    )
    preact = conv(x_pad, w_one.reshape(3, 3, inner, chan_full), 0, "HWOI") + bias_one
    hidden = smooth_gate(preact).astype(jnp.bfloat16)
    h_pad = with_frame(hidden, picked(swap(to_send(hidden))))
    partial = conv(h_pad, w_two.reshape(3, 3, chan_full, inner), 0, "HWOI").reshape(
        cells, chan_full
    )
    mixed = partial
    rounded = partial.astype(jnp.bfloat16)
    for shift in range(1, chans):
        mixed = mixed + lax.ppermute(
            rounded, "chan", [(i, (i + shift) % chans) for i in range(chans)]
        ).astype(jnp.float32)
    x_flat = x_grid.reshape(cells, chan_full)
    misfit = x_flat.astype(jnp.float32) + mixed - target_patch.astype(jnp.float32)
    weighted = lat_w * misfit
    loss_local = jnp.sum(weighted * misfit)
    inv_root = 1.0 / math.sqrt(count * cells)
    grad_out = (weighted * inv_root).astype(jnp.bfloat16)
    g_grid = grad_out.reshape(length, length, chan_full)
    h_taps = [
        h_pad[a : a + length, b : b + length].reshape(cells, inner)
        for a in range(3)
        for b in range(3)
    ]
    two_local = jnp.stack(
        [
            lax.dot_general(
                grad_out, tap, (((0,), (0,)), ((), ())), preferred_element_type=jnp.float32
            )
            for tap in h_taps
        ]
    )
    near = picked(swap(to_send(g_grid)))
    side_taps = jnp.array([[0, 1, 2], [6, 7, 8], [0, 3, 6], [2, 5, 8]], jnp.int32)
    used = side_taps[own_code % 4]
    used = jnp.where((own_code >= 4)[:, None], used[:, ::-1], used)
    hot = (used[:, :, None] == jnp.arange(9)[None, None, :]).astype(jnp.bfloat16)
    spread = jnp.pad(near, ((0, 0), (1, 1), (0, 0)))
    shifted = jnp.stack([spread[:, 2 - d : 2 - d + length] for d in range(3)], axis=1)
    side_in = jnp.einsum("tdn,tdkc->tknc", hot, shifted, preferred_element_type=jnp.float32).astype(
        jnp.bfloat16
    )
    back = lax.dot_general(
        side_in.reshape(4 * length, 9 * chan_full),
        w_two.reshape(9 * chan_full, inner),
        (((1,), (0,)), ((), ())),
        preferred_element_type=jnp.float32,
    ).reshape(4, length, inner)
    grad_h = conv(g_grid, w_two.reshape(3, 3, chan_full, inner)[::-1, ::-1], 1, "HWIO")
    row = lax.broadcasted_iota(jnp.int32, (length, length, 1), 0)
    col = lax.broadcasted_iota(jnp.int32, (length, length, 1), 1)
    grad_h = (
        grad_h
        + jnp.where(row == 0, back[0][None], 0.0)
        + jnp.where(row == length - 1, back[1][None], 0.0)
        + jnp.where(col == 0, back[2][:, None], 0.0)
        + jnp.where(col == length - 1, back[3][:, None], 0.0)
    )
    grad_pre = jax.vjp(smooth_gate, preact)[1](grad_h)[0].reshape(cells, inner)
    bias_local = jnp.sum(grad_pre, axis=0)
    pre_b = grad_pre.astype(jnp.bfloat16)
    x_taps = [
        x_pad[a : a + length, b : b + length].reshape(cells, chan_full)
        for a in range(3)
        for b in range(3)
    ]
    one_local = jnp.stack(
        [
            lax.dot_general(
                pre_b, tap, (((0,), (0,)), ((), ())), preferred_element_type=jnp.float32
            )
            for tap in x_taps
        ]
    )
    small_rows = -(-inner // chan_full) + 1
    small = jnp.concatenate(
        [
            jnp.pad(bias_local, (0, (small_rows - 1) * chan_full - inner)),
            jnp.pad(loss_local[None], (0, chan_full - 1)),
        ]
    ).reshape(small_rows, chan_full)
    sum_two = lax.psum(two_local, "patch")
    sums = lax.psum(
        jnp.concatenate([one_local.reshape(9 * inner, chan_full), small], axis=0), "patch"
    )
    grad_one = sums[: 9 * inner].reshape(9, inner, chan_full)
    grad_bias = sums[9 * inner : -1].reshape(-1)[:inner]
    loss_value = sums[-1, 0] / (count * cells * chan_full)
    return (loss_value, grad_one, sum_two, grad_bias)


def solution(mesh):
    placed = (
        P("patch", "chan", None),
        P(None, "chan", None),
        P("chan"),
        P(None, None, "chan"),
        P(),
        P(),
        P(),
        P("patch", "chan", None),
        P("patch", None),
    )
    return jax.shard_map(
        on_device,
        mesh=mesh,
        in_specs=placed,
        out_specs=(P(), P(None, "chan", None), P(None, None, "chan"), P("chan")),
        check_vma=False,
    )
```

profile of v0, /device:TPU:0, one launch (start us, length us, event | category | flops | bytes accessed | tf_op | source)
XLA Modules:
  0.0 233.3 jit_solution(5168928998311883322)
XLA Ops:
  7.2 1.2 copy.213
  8.4 1.1 copy.214
  9.5 0.6 pad_maximum_fusion.8
  10.1 9.9 %all_gather.3 = bf16[2,128,1024]{2,0,1:T(2,128)(2,1)S(1)} all-gather(bf16[2,64,1024]{2,0,1:T(2,128)(2,1)S(1)} %pad_maximum_fusion.8), channel_id=1, replica_groups=mesh['patch'=16,'chan'=2] {'chan'}, dimensions={1}, use_global_device_ids=true | all-gather | bytes 786432 | tf_op jit(solution)/shard_map/all_gather | solution.py:65
  20.0 0.7 fusion.121
  20.7 0.4 copy.274
  21.7 0.4 copy.275
  23.2 0.9 copy.219
  24.0 6.2 %all-to-all-start = ((bf16[16,97,128]{2,1,0:T(8,128)(2,1)}), bf16[16,97,128]{2,1,0:T(8,128)(2,1)S(1)}, u32[]{:S(2)}, u32[]{:S(2)}) async-start(bf16[16,97,128]{2,1,0:T(8,128)(2,1)} %copy.219), calls=%async_computation | async-start | bytes 851968 | tf_op jit(solution)/shard_map/all_to_all | solution.py:63
  30.3 0.6 gather_fusion
  30.9 0.6 iota_compare_fusion.7
  31.5 0.7 broadcast_select_fusion.3
  32.2 10.8 %all-to-all-done = bf16[16,97,128]{2,1,0:T(8,128)(2,1)S(1)} async-done(((bf16[16,97,128]{2,1,0:T(8,128)(2,1)}), bf16[16,97,128]{2,1,0:T(8,128)(2,1)S(1)}, u32[]{:S(2)}, u32[]{:S(2)}) %all-to-all-start) | async-done | bytes 397344 | tf_op jit(solution)/shard_map/all_to_all | solution.py:63
  44.3 2.3 subtract_multiply_fusion
  47.5 1.0 slice.267
  48.5 1.4 add_multiply_fusion
  50.0 1.5 copy.250
  51.7 0.9 pad_maximum_fusion.6
  52.7 0.8 broadcast_select_fusion
  53.9 0.8 copy.233
  54.7 4.4 %all-to-all-start.1 = ((bf16[16,32,256]{2,1,0:T(8,128)(2,1)}), bf16[16,32,256]{2,1,0:T(8,128)(2,1)}, u32[]{:S(2)}, u32[]{:S(2)}) async-start(bf16[16,32,256]{2,1,0:T(8,128)(2,1)} %copy.233), calls=%async_computation.1 | async-start | bytes 524288 | tf_op jit(solution)/shard_map/all_to_all | solution.py:63
  59.1 0.8 slice.259
  59.9 1.9 copy.262
  61.9 1.5 copy.249
  63.4 1.5 copy.252
  64.8 1.5 copy.251
  66.3 1.0 fusion.123
  67.3 1.0 fusion.122
  68.3 1.1 fusion.38
  69.4 1.2 convolution_convert_fusion.5
  70.8 0.5 pad_maximum_fusion.1
  71.7 0.4 pad_maximum_fusion.2
  73.2 0.8 copy-done.19
  74.0 1.7 convolution_select_fusion.2
  76.2 1.6 collective-permute-start
  78.5 1.1 copy.260
  79.5 1.1 copy.261
  81.6 1.1 copy.266
  82.7 1.9 collective-permute-done
  84.6 0.8 fusion.58
  85.4 0.9 fusion.13
  86.7 1.0 convolution_select_fusion
  87.7 1.7 copy.242
  89.9 0.7 copy.246
  90.6 5.9 %all-to-all-start.2 = ((bf16[16,32,128]{2,1,0:T(8,128)(2,1)}), bf16[16,32,128]{2,1,0:T(8,128)(2,1)}, u32[]{:S(2)}, u32[]{:S(2)}) async-start(bf16[16,32,128]{2,1,0:T(8,128)(2,1)} %copy.246), calls=%async_computation.2 | async-start | bytes 262144 | tf_op jit(solution)/shard_map/all_to_all | solution.py:63
  96.5 0.9 fusion.12
  97.5 2.0 fusion.11
  99.4 0.9 fusion.10
  100.4 0.9 fusion.9
  101.3 0.9 fusion.8
  102.2 0.9 fusion.7
  103.1 0.9 fusion.6
  104.1 0.9 fusion.5
  105.0 1.2 convolution_convert_fusion.6
  106.4 0.4 convolution_convert_fusion
  106.8 1.3 fusion.74
  108.2 3.8 %fusion.116 = (bf16[1,32,32,256]{3,1,2,0:T(8,128)(2,1)S(1)}, f32[1,32,32,256]{3,1,2,0:T(8,128)}) fusion(f32[32,1,40,256]{3,0,2,1:T(8,128)} %bitcast.352, f32[32,1,40,256]{3,0,2,1:T(8,128)} %bitcast.353, f32[32,1,40,256]{3,0,2,1:T(8,128)S(1)} %bitcast.350, f32[32,1,40,256]{3,0,2,1:T(8,128)S(1)} %bitcast.351, f32[32,256]{1,0:T(8,128)S(1)} %get-tuple-element.49, ...), kind=kLoop, calls=%fused_computation.217 | loop fusion | flops 4718592 | bytes 6948864 | tf_op jit(solution)/shard_map/convert_element_type | solution.py:146
  116.1 0.7 fusion.99
  116.8 1.1 pad_maximum_fusion
  117.9 100.8 %all-reduce.10.cloned.1.call-done = (f32[2307,128]{1,0:T(8,128)}, f32[9,128,256]{2,1,0:T(8,128)}) async-done(((f32[2307,128]{1,0:T(8,128)}, f32[9,128,256]{2,1,0:T(8,128)}), (f32[2307,128]{1,0:T(8,128)}, f32[9,128,256]{2,1,0:T(8,128)})) %all-reduce.10.cloned.1.call-update) | async-done | bytes 2360848 | tf_op jit(solution)/shard_map/psum | solution.py:168
  218.8 2.5 %slice.300 = f32[2304,128]{1,0:T(8,128)} slice(f32[2307,128]{1,0:T(8,128)} %get-tuple-element.4), slice={[0:2304], [0:128]} | slice | bytes 2359296 | tf_op jit(solution)/shard_map/slice | solution.py:171
  221.2 1.2 slice.299
  222.4 1.2 slice_bitcast_fusion.13
  224.3 1.0 copy.337
  (166 shorter events, 12.9 us)
Async XLA Ops:
  7.2 36.7 %copy-start = (bf16[9,256,128]{2,1,0:T(8,128)(2,1)S(1)}, bf16[9,256,128]{2,1,0:T(8,128)(2,1)}, u32[]{:S(2)}) copy-start(bf16[9,256,128]{2,1,0:T(8,128)(2,1)} %param.11) | copy-start | bytes 1769476
  20.0 1.3 copy-start.24
  20.0 1.5 copy-start.30
  20.7 1.7 copy-start.25
  20.7 2.2 copy-start.31
  23.1 7.2 %copy-start.22 = (s32[4,3]{1,0:T(4,128)S(1)}, s32[4,3]{1,0:T(4,128)}, u32[]{:S(2)}) copy-start(s32[4,3]{1,0:T(4,128)} %constant.54.clone) | copy-start | bytes 148
  24.0 18.9 %all-to-all-start = ((bf16[16,97,128]{2,1,0:T(8,128)(2,1)}), bf16[16,97,128]{2,1,0:T(8,128)(2,1)S(1)}, u32[]{:S(2)}, u32[]{:S(2)}) async-start(bf16[16,97,128]{2,1,0:T(8,128)(2,1)} %copy.219), calls=%async_computation | async-start | bytes 851968 | tf_op jit(solution)/shard_map/all_to_all | solution.py:63
  43.0 0.8 copy-start.8
  43.6 0.7 copy-start.26
  43.6 0.7 copy-start.32
  47.5 5.1 %copy-start.20 = (bf16[1,32,256]{2,1,0:T(8,128)(2,1)}, bf16[1,32,256]{2,1,0:T(8,128)(2,1)S(1)}, u32[]{:S(2)}) copy-start(bf16[1,32,256]{2,1,0:T(8,128)(2,1)S(1)} %get-tuple-element.26) | copy-start | bytes 49156
  47.5 5.1 %copy-start.21 = (bf16[1,32,256]{2,1,0:T(8,128)(2,1)}, bf16[1,32,256]{2,1,0:T(8,128)(2,1)S(1)}, u32[]{:S(2)}) copy-start(bf16[1,32,256]{2,1,0:T(8,128)(2,1)S(1)} %get-tuple-element.27) | copy-start | bytes 49156
  54.7 14.8 %all-to-all-start.1 = ((bf16[16,32,256]{2,1,0:T(8,128)(2,1)}), bf16[16,32,256]{2,1,0:T(8,128)(2,1)}, u32[]{:S(2)}, u32[]{:S(2)}) async-start(bf16[16,32,256]{2,1,0:T(8,128)(2,1)} %copy.233), calls=%async_computation.1 | async-start | bytes 524288 | tf_op jit(solution)/shard_map/all_to_all | solution.py:63
  59.9 1.9 copy-start.1
  63.4 1.5 copy-start.9
  67.3 1.0 copy-start.27
  72.9 1.1 copy-start.19
  72.9 1.1 copy-start.33
  76.2 8.3 %collective-permute-start = (bf16[1024,128]{1,0:T(8,128)(2,1)S(1)}, bf16[1024,128]{1,0:T(8,128)(2,1)S(1)}, u32[]{:S(2)}, u32[]{:S(2)}) collective-permute-start(bf16[1024,128]{1,0:T(8,128)(2,1)S(1)} %bitcast_convert_fusion), channel_id=1, source_target_pairs={{0,1},{1,0},{2,3},{3,2},{4,5},{5,4},{6,7},{7,6},{8,9},{9,8},{10,11... | collective-permute-start | bytes 786440 | tf_op jit(solution)/shard_map/ppermute | solution.py:95
  81.3 3.3 %slice-start = ((bf16[16,97,128]{2,1,0:T(8,128)(2,1)}), bf16[16,64,128]{2,1,0:T(8,128)(2,1)S(1)}, s32[]{:S(2)}) async-start(bf16[16,97,128]{2,1,0:T(8,128)(2,1)} %copy-done.8), calls=%async_computation.4 | async-start | bytes 524288 | tf_op jit(solution)/shard_map/slice | solution.py:79
  90.6 14.4 %all-to-all-start.2 = ((bf16[16,32,128]{2,1,0:T(8,128)(2,1)}), bf16[16,32,128]{2,1,0:T(8,128)(2,1)}, u32[]{:S(2)}, u32[]{:S(2)}) async-start(bf16[16,32,128]{2,1,0:T(8,128)(2,1)} %copy.246), calls=%async_computation.2 | async-start | bytes 262144 | tf_op jit(solution)/shard_map/all_to_all | solution.py:63
  96.4 122.3 %all-reduce.10.cloned.1.call-start = ((), (), s32[]{:S(2)}) async-start(), calls=%async_computation.3 | async-start | bytes 4726784 | tf_op jit(solution)/shard_map/psum | solution.py:168
  96.5 2.9 %copy-start.6 = (bf16[32,32,256]{2,1,0:T(8,128)(2,1)S(1)}, bf16[32,32,256]{2,1,0:T(8,128)(2,1)}, u32[]{:S(2)}) copy-start(bf16[32,32,256]{2,1,0:T(8,128)(2,1)} %copy.261) | copy-start | bytes 1572868
  96.5 3.8 %copy-start.7 = (bf16[1024,256]{1,0:T(8,128)(2,1)S(1)}, bf16[1024,256]{1,0:T(8,128)(2,1)}, u32[]{:S(2)}) copy-start(bf16[1024,256]{1,0:T(8,128)(2,1)} %fusion.38) | copy-start | bytes 1572868
  101.3 2.8 %copy-start.5 = (bf16[32,32,256]{2,1,0:T(8,128)(2,1)S(1)}, bf16[32,32,256]{2,1,0:T(8,128)(2,1)}, u32[]{:S(2)}) copy-start(bf16[32,32,256]{2,1,0:T(8,128)(2,1)} %copy.266) | copy-start | bytes 1572868
  103.1 3.2 %copy-start.23 = (s32[4,3]{1,0:T(4,128)S(1)}, s32[4,3]{1,0:T(4,128)}, u32[]{:S(2)}) copy-start(s32[4,3]{1,0:T(4,128)} %broadcast_select_fusion.3) | copy-start | bytes 148
  104.1 4.1 %copy-start.3 = (f32[32,8,5,256]{3,0,2,1:T(8,128)S(1)}, f32[32,8,5,256]{3,0,2,1:T(8,128)}, u32[]{:S(2)}) copy-start(f32[32,8,5,256]{3,0,2,1:T(8,128)} %copy.249) | copy-start | bytes 3932164
  105.0 3.1 %copy-start.2 = (f32[32,8,5,256]{3,0,2,1:T(8,128)S(1)}, f32[32,8,5,256]{3,0,2,1:T(8,128)}, u32[]{:S(2)}) copy-start(f32[32,8,5,256]{3,0,2,1:T(8,128)} %copy.250) | copy-start | bytes 3932164
  105.0 3.1 %copy-start.28 = (pred[32]{0:T(512)(128)(4,1)S(1)}, pred[32]{0:T(512)(128)(4,1)}, u32[]{:S(2)}) copy-start(pred[32]{0:T(512)(128)(4,1)} %get-tuple-element.67) | copy-start | bytes 100
  105.0 3.2 %copy-start.29 = (pred[32]{0:T(512)(128)(4,1)S(1)}, pred[32]{0:T(512)(128)(4,1)}, u32[]{:S(2)}) copy-start(pred[32]{0:T(512)(128)(4,1)} %get-tuple-element.68) | copy-start | bytes 100
  108.2 4.1 %copy-start.17 = (bf16[32,32,128]{2,1,0:T(8,128)(2,1)S(1)}, bf16[32,32,128]{2,1,0:T(8,128)(2,1)}, u32[]{:S(2)}) copy-start(bf16[32,32,128]{2,1,0:T(8,128)(2,1)} %get-tuple-element.35) | copy-start | bytes 786436
  111.9 0.9 copy-start.12
  112.0 1.3 copy-start.18
  112.3 1.3 copy-start.15
  113.3 1.1 copy-start.16
  113.6 1.1 copy-start.13
  114.0 1.1 copy-start.11
  114.3 1.1 copy-start.14
  114.7 1.3 copy-start.4
  218.8 5.5 %copy-start.10 = (f32[9,128,256]{2,1,0:T(8,128)S(1)}, f32[9,128,256]{2,1,0:T(8,128)}, u32[]{:S(2)}) copy-start(f32[9,128,256]{2,1,0:T(8,128)} %get-tuple-element.71) | copy-start | bytes 3538948
Sparse Core Ops, SparseCore 0:
  118.0 100.6 all-reduce.9
where the time goes:
time: 234 us; the launch traced here: 233 us
  waiting for transfers between devices  114 us (49%)
  local copies, waits for them, and re-layouts  36.7 us (16%)
  matrix products  23.1 us (10%)
  starting transfers between devices  18 us (8%)
  between operations  16.8 us (7%)
  other arithmetic  15.3 us (7%)
  blocking collectives  9.91 us (4%)
    psum x1, waiting for transfers between devices, on_device(): lax.psum(jnp.concatenate([one_local.reshape(9 * inner, chan_full), small]...  101 us
    all_to_all x3, starting transfers between devices, swap(): lax.all_to_all(sent, 'patch', split_axis=0, concat_axis=0, tiled=True)  16.4 us
    all_to_all x3, waiting for transfers between devices, swap(): lax.all_to_all(sent, 'patch', split_axis=0, concat_axis=0, tiled=True)  10.8 us
    all_gather x1, blocking collectives, on_device(): lax.all_gather(jnp.stack([fields[0], target[0]]), 'chan', axis=1, tiled=T...  9.91 us
    dot_general x9, matrix products, on_device(): lax.dot_general(grad_out, tap, (((0,), (0,)), ((), ())), preferred_elemen...  9.39 us
    unnamed x85, local copies, waits for them, and re-layouts  6.32 us
    conv_general_dilated x13, local copies, waits for them, and re-layouts, conv(): lax.conv_general_dilated(values[None], weight, (1, 1), ((pad, pad), (pad,...  6.06 us
    slice x10, local copies, waits for them, and re-layouts, on_device(): h_pad[a:a + length, b:b + length].reshape(cells, inner)  5.55 us
  transfers between devices with their start and end apart: 5, of which 3 were waited for; matrix products, arithmetic and copies ran while one was open for 11% of the time, Pallas kernels for 0%

commit v1 on v0

--- a/solution.py
+++ b/solution.py
@@ -165,9 +165,9 @@
         ]
     ).reshape(small_rows, chan_full)
     sum_two = lax.psum(two_local, "patch")
-    sums = lax.psum(
-        jnp.concatenate([one_local.reshape(9 * inner, chan_full), small], axis=0), "patch"
-    )
+    x = jnp.concatenate([one_local.reshape(9 * inner, chan_full), small], axis=0)
+    blocks = lax.all_gather(x, "patch")
+    sums = jnp.sum(blocks, axis=0)
     grad_one = sums[: 9 * inner].reshape(9, inner, chan_full)
     grad_bias = sums[9 * inner : -1].reshape(-1)[:inner]
     loss_value = sums[-1, 0] / (count * cells * chan_full)

time: 234 us -> 318 us (1.36)
  waiting for transfers between devices: 114 us -> 189 us
  other arithmetic: 15.3 us -> 25.5 us
    all_gather x0 -> x1, waiting for transfers between devices: none -> 81.8 us  [on_device(): blocks = lax.all_gather(x, 'patch')]
    psum x1, waiting for transfers between devices: 101 us -> 87.5 us  [on_device(): sum_two = lax.psum(two_local, 'patch')]
    all_to_all x3, waiting for transfers between devices: 10.8 us -> 20 us  [swap(): lax.all_to_all(sent, 'patch', split_axis=0, concat_axis=0, tiled=True)]
    reduce_sum x0 -> x1, other arithmetic: none -> 7.38 us  [on_device(): sums = jnp.sum(blocks, axis=0)]
    unnamed x85 -> x111, local copies, waits for them, and re-layouts: 6.32 us -> 11 us
  transfers between devices with their start and end apart: 5 -> 6, of which waited for: 3 -> 5; matrix products, arithmetic and copies ran while one was open for 11% -> 13% of each run, Pallas kernels for 0% -> 0%
where the time goes in v1:
time: 318 us; the launch traced here: 317 us
  waiting for transfers between devices  189 us (59%)
  local copies, waits for them, and re-layouts  37.2 us (12%)
  other arithmetic  25.5 us (8%)
  matrix products  21.6 us (7%)
  between operations  16.9 us (5%)
  starting transfers between devices  16.1 us (5%)
  blocking collectives  9.91 us (3%)
    psum x1, waiting for transfers between devices, on_device(): sum_two = lax.psum(two_local, 'patch')  87.5 us
    all_gather x1, waiting for transfers between devices, on_device(): blocks = lax.all_gather(x, 'patch')  81.8 us
    all_to_all x3, waiting for transfers between devices, swap(): lax.all_to_all(sent, 'patch', split_axis=0, concat_axis=0, tiled=True)  20 us
    all_to_all x3, starting transfers between devices, swap(): lax.all_to_all(sent, 'patch', split_axis=0, concat_axis=0, tiled=True)  14.1 us
    unnamed x111, local copies, waits for them, and re-layouts  11 us
    all_gather x1, blocking collectives, on_device(): lax.all_gather(jnp.stack([fields[0], target[0]]), 'chan', axis=1, tiled=T...  9.91 us
    dot_general x9, matrix products, on_device(): lax.dot_general(grad_out, tap, (((0,), (0,)), ((), ())), preferred_elemen...  8.39 us
    reduce_sum x1, other arithmetic, on_device(): sums = jnp.sum(blocks, axis=0)  7.38 us
  transfers between devices with their start and end apart: 6, of which 5 were waited for; matrix products, arithmetic and copies ran while one was open for 13% of the time, Pallas kernels for 0%

profile of v1, /device:TPU:0, one launch (start us, length us, event | category | flops | bytes accessed | tf_op | source)
XLA Modules:
  0.0 316.6 jit_solution(12755892531535980469)
XLA Ops:
  7.2 1.2 copy.213
  8.4 1.1 copy.214
  9.5 0.6 pad_maximum_fusion.7
  10.1 9.9 %all_gather.9 = bf16[2,128,1024]{2,0,1:T(2,128)(2,1)S(1)} all-gather(bf16[2,64,1024]{2,0,1:T(2,128)(2,1)S(1)} %pad_maximum_fusion.7), channel_id=1, replica_groups=mesh['patch'=16,'chan'=2] {'chan'}, dimensions={1}, use_global_device_ids=true | all-gather | bytes 786432 | tf_op jit(solution)/shard_map/all_gather | solution.py:65
  20.0 0.7 fusion.121
  23.2 0.9 copy.219
  24.1 6.2 %all-to-all-start = ((bf16[16,97,128]{2,1,0:T(8,128)(2,1)}), bf16[16,97,128]{2,1,0:T(8,128)(2,1)S(1)}, u32[]{:S(2)}, u32[]{:S(2)}) async-start(bf16[16,97,128]{2,1,0:T(8,128)(2,1)} %copy.219), calls=%async_computation | async-start | bytes 851968 | tf_op jit(solution)/shard_map/all_to_all | solution.py:63
  30.3 0.6 gather_fusion
  31.0 0.6 iota_compare_fusion.7
  31.6 0.7 broadcast_select_fusion.3
  32.2 10.8 %all-to-all-done = bf16[16,97,128]{2,1,0:T(8,128)(2,1)S(1)} async-done(((bf16[16,97,128]{2,1,0:T(8,128)(2,1)}), bf16[16,97,128]{2,1,0:T(8,128)(2,1)S(1)}, u32[]{:S(2)}, u32[]{:S(2)}) %all-to-all-start) | async-done | bytes 397344 | tf_op jit(solution)/shard_map/all_to_all | solution.py:63
  44.0 0.5 copy-done.39
  44.4 2.4 subtract_multiply_fusion
  47.7 1.1 pad_maximum_fusion.4
  48.8 0.6 copy-done.24
  49.5 0.8 broadcast_select_fusion
  50.4 1.0 convolution_convert_fusion.2
  51.4 0.8 copy.233
  52.2 4.4 %all-to-all-start.1 = ((bf16[16,32,256]{2,1,0:T(8,128)(2,1)}), bf16[16,32,256]{2,1,0:T(8,128)(2,1)}, u32[]{:S(2)}, u32[]{:S(2)}) async-start(bf16[16,32,256]{2,1,0:T(8,128)(2,1)} %copy.233), calls=%async_computation.1 | async-start | bytes 524288 | tf_op jit(solution)/shard_map/all_to_all | solution.py:63
  56.6 0.8 slice.259
  57.3 2.2 fusion.123
  59.5 1.9 add_multiply_fusion
  61.4 5.1 %all-to-all-done.1 = bf16[16,32,256]{2,1,0:T(8,128)(2,1)} async-done(((bf16[16,32,256]{2,1,0:T(8,128)(2,1)}), bf16[16,32,256]{2,1,0:T(8,128)(2,1)}, u32[]{:S(2)}, u32[]{:S(2)}) %all-to-all-start.1) | async-done | bytes 262176 | tf_op jit(solution)/shard_map/all_to_all | solution.py:63
  66.4 1.2 convolution_convert_fusion.5
  68.6 0.8 copy-done.18
  69.5 1.7 convolution_select_fusion.2
  71.7 0.8 copy-done.3
  72.5 0.8 bitcast_convert_fusion
  73.3 1.5 collective-permute-start
  74.8 0.9 pad_maximum_fusion.5
  75.7 1.5 copy.250
  77.2 2.9 copy.249
  80.1 1.5 copy.252
  81.6 1.5 copy.251
  83.1 1.0 fusion.122
  84.5 1.8 fusion.58
  86.6 0.7 slice.279
  87.8 0.7 copy.246
  88.5 3.5 %all-to-all-start.2 = ((bf16[16,32,128]{2,1,0:T(8,128)(2,1)}), bf16[16,32,128]{2,1,0:T(8,128)(2,1)S(1)}, u32[]{:S(2)}, u32[]{:S(2)}) async-start(bf16[16,32,128]{2,1,0:T(8,128)(2,1)} %copy.246), calls=%async_computation.2 | async-start | bytes 262144 | tf_op jit(solution)/shard_map/all_to_all | solution.py:63
  92.3 1.9 convolution_select_fusion
  94.2 1.5 copy.242
  95.7 4.2 %all-to-all-done.2 = bf16[16,32,128]{2,1,0:T(8,128)(2,1)S(1)} async-done(((bf16[16,32,128]{2,1,0:T(8,128)(2,1)}), bf16[16,32,128]{2,1,0:T(8,128)(2,1)S(1)}, u32[]{:S(2)}, u32[]{:S(2)}) %all-to-all-start.2) | async-done | bytes 131104 | tf_op jit(solution)/shard_map/all_to_all | solution.py:63
  101.2 3.1 fusion.116
  108.1 1.0 copy-done.8
  109.3 0.7 fusion.99
  110.0 2.4 maximum_bitcast_fusion
  112.8 0.6 copy.262
  114.2 0.5 pad_maximum_fusion
  118.3 0.9 fusion.13
  119.2 0.9 fusion.12
  120.2 0.9 fusion.11
  121.1 0.9 fusion.10
  122.0 0.9 fusion.9
  123.0 0.9 fusion.8
  123.9 0.9 fusion.7
  124.8 0.9 fusion.6
  125.8 0.9 fusion.5
  126.7 81.8 %all-gather.4.cloned.1.call-done = f32[16,2307,128]{2,1,0:T(8,128)} async-done(((f32[1,2307,128]{2,1,0:T(8,128)}), f32[16,2307,128]{2,1,0:T(8,128)}) %all-gather.4.cloned.1.call-update) | async-done | bytes 18898960 | tf_op jit(solution)/shard_map/all_gather | solution.py:169
  208.5 7.4 %reduce_sum.29 = f32[2307,128]{1,0:T(8,128)S(1)} reduce(f32[16,2307,128]{2,1,0:T(8,128)} %all-gather.4.cloned.1.call-done, f32[]{:T(128)} %constant.49.clone.1), dimensions={0}, to_apply=%region_2.3 | reduce | flops 4429440 | bytes 20080132 | tf_op jit(solution)/shard_map/reduce_sum | solution.py:170
  215.9 1.1 slice.300
  217.0 0.5 slice.299
  218.2 0.6 slice_bitcast_fusion.13
  218.7 87.5 %all-reduce.9.cloned.1.call-done = f32[9,128,256]{2,1,0:T(8,128)} async-done(((f32[9,128,256]{2,1,0:T(8,128)}), f32[9,128,256]{2,1,0:T(8,128)}) %all-reduce.9.cloned.1.call-update) | async-done | bytes 1179664 | tf_op jit(solution)/shard_map/psum | solution.py:167
  306.2 2.4 copy.336
  (196 shorter events, 17.0 us)
Async XLA Ops:
  7.2 36.8 %copy-start = (bf16[9,256,128]{2,1,0:T(8,128)(2,1)S(1)}, bf16[9,256,128]{2,1,0:T(8,128)(2,1)}, u32[]{:S(2)}) copy-start(bf16[9,256,128]{2,1,0:T(8,128)(2,1)} %param.11) | copy-start | bytes 1769476
  20.0 1.3 copy-start.37
  20.0 1.5 copy-start.43
  20.7 1.7 copy-start.38
  20.7 2.2 copy-start.44
  21.5 10.0 %copy-start.34 = (pred[4]{0:T(512)(128)(4,1)}, pred[4]{0:T(512)(128)(4,1)S(1)}, u32[]{:S(2)}) copy-start(pred[4]{0:T(512)(128)(4,1)S(1)} %compare_reduce_fusion) | copy-start | bytes 16
  21.7 21.3 %copy-start.32 = (s32[4]{0:T(128)}, s32[4]{0:T(128)S(1)}, u32[]{:S(2)}) copy-start(s32[4]{0:T(128)S(1)} %get-tuple-element.63) | copy-start | bytes 52
  23.1 7.2 %copy-start.31 = (s32[4,3]{1,0:T(4,128)S(1)}, s32[4,3]{1,0:T(4,128)}, u32[]{:S(2)}) copy-start(s32[4,3]{1,0:T(4,128)} %constant.54.clone) | copy-start | bytes 148
  24.1 18.9 %all-to-all-start = ((bf16[16,97,128]{2,1,0:T(8,128)(2,1)}), bf16[16,97,128]{2,1,0:T(8,128)(2,1)S(1)}, u32[]{:S(2)}, u32[]{:S(2)}) async-start(bf16[16,97,128]{2,1,0:T(8,128)(2,1)} %copy.219), calls=%async_computation | async-start | bytes 851968 | tf_op jit(solution)/shard_map/all_to_all | solution.py:63
  43.0 0.8 copy-start.7
  43.3 4.4 %copy-start.27 = (bf16[1,32,128]{2,1,0:T(8,128)(2,1)}, bf16[1,32,128]{2,1,0:T(8,128)(2,1)S(1)}, u32[]{:S(2)}) copy-start(bf16[1,32,128]{2,1,0:T(8,128)(2,1)S(1)} %copy.222) | copy-start | bytes 24580
  43.3 4.4 %copy-start.29 = (bf16[1,32,128]{2,1,0:T(8,128)(2,1)}, bf16[1,32,128]{2,1,0:T(8,128)(2,1)S(1)}, u32[]{:S(2)}) copy-start(bf16[1,32,128]{2,1,0:T(8,128)(2,1)S(1)} %copy.223) | copy-start | bytes 24580
  43.8 0.7 copy-start.39
  43.8 0.7 copy-start.45
  47.7 1.1 copy-start.25
  47.7 1.1 copy-start.26
  48.8 0.6 copy-start.24
  52.2 14.2 %all-to-all-start.1 = ((bf16[16,32,256]{2,1,0:T(8,128)(2,1)}), bf16[16,32,256]{2,1,0:T(8,128)(2,1)}, u32[]{:S(2)}, u32[]{:S(2)}) async-start(bf16[16,32,256]{2,1,0:T(8,128)(2,1)} %copy.233), calls=%async_computation.1 | async-start | bytes 524288 | tf_op jit(solution)/shard_map/all_to_all | solution.py:63
  59.5 6.9 %copy-start.33 = (s32[4]{0:T(128)S(1)}, s32[4]{0:T(128)}, u32[]{:S(2)}) copy-start(s32[4]{0:T(128)} %copy-done.32) | copy-start | bytes 52
  67.8 0.6 copy-start.20
  67.8 0.6 copy-start.22
  68.4 1.1 copy-start.18
  68.4 1.1 copy-start.46
  71.4 3.4 %copy-start.28 = (bf16[1,32,128]{2,1,0:T(8,128)(2,1)S(1)}, bf16[1,32,128]{2,1,0:T(8,128)(2,1)}, u32[]{:S(2)}) copy-start(bf16[1,32,128]{2,1,0:T(8,128)(2,1)} %copy-done.27) | copy-start | bytes 24580
  71.4 3.4 %copy-start.30 = (bf16[1,32,128]{2,1,0:T(8,128)(2,1)S(1)}, bf16[1,32,128]{2,1,0:T(8,128)(2,1)}, u32[]{:S(2)}) copy-start(bf16[1,32,128]{2,1,0:T(8,128)(2,1)} %copy-done.29) | copy-start | bytes 24580
  71.7 0.8 copy-start.3
  73.3 10.8 %collective-permute-start = (bf16[1024,128]{1,0:T(8,128)(2,1)}, bf16[1024,128]{1,0:T(8,128)(2,1)}, u32[]{:S(2)}, u32[]{:S(2)}) collective-permute-start(bf16[1024,128]{1,0:T(8,128)(2,1)} %bitcast_convert_fusion), channel_id=1, source_target_pairs={{0,1},{1,0},{2,3},{3,2},{4,5},{5,4},{6,7},{7,6},{8,9},{9,8},{10,11... | collective-permute-start | bytes 786440 | tf_op jit(solution)/shard_map/ppermute | solution.py:95
  77.2 2.9 copy-start.2
  80.1 1.5 copy-start.9
  81.6 1.5 copy-start.6
  83.1 1.2 copy-start.4
  83.1 1.4 slice-start
  86.3 1.1 copy-start.35
  86.4 5.9 %copy-start.19 = (bf16[9,128,256]{2,1,0:T(8,128)(2,1)S(1)}, bf16[9,128,256]{2,1,0:T(8,128)(2,1)}, u32[]{:S(2)}) copy-start(bf16[9,128,256]{2,1,0:T(8,128)(2,1)} %param.13) | copy-start | bytes 1769476
  88.5 11.4 %all-to-all-start.2 = ((bf16[16,32,128]{2,1,0:T(8,128)(2,1)}), bf16[16,32,128]{2,1,0:T(8,128)(2,1)S(1)}, u32[]{:S(2)}, u32[]{:S(2)}) async-start(bf16[16,32,128]{2,1,0:T(8,128)(2,1)} %copy.246), calls=%async_computation.2 | async-start | bytes 262144 | tf_op jit(solution)/shard_map/all_to_all | solution.py:63
  92.0 116.5 %all-gather.4.cloned.1.call-start = ((), (), s32[]{:S(2)}) async-start(), calls=%async_computation.4 | async-start | bytes 20123648 | tf_op jit(solution)/shard_map/all_gather | solution.py:169
  94.2 6.0 %copy-start.36 = (s32[4,3]{1,0:T(4,128)S(1)}, s32[4,3]{1,0:T(4,128)}, u32[]{:S(2)}) copy-start(s32[4,3]{1,0:T(4,128)} %broadcast_select_fusion.3) | copy-start | bytes 148
  95.7 5.2 %copy-start.41 = (pred[32]{0:T(512)(128)(4,1)S(1)}, pred[32]{0:T(512)(128)(4,1)}, u32[]{:S(2)}) copy-start(pred[32]{0:T(512)(128)(4,1)} %get-tuple-element.65) | copy-start | bytes 100
  95.7 5.3 %copy-start.42 = (pred[32]{0:T(512)(128)(4,1)S(1)}, pred[32]{0:T(512)(128)(4,1)}, u32[]{:S(2)}) copy-start(pred[32]{0:T(512)(128)(4,1)} %get-tuple-element.66) | copy-start | bytes 100
  99.9 1.3 copy-start.5
  101.2 3.5 %copy-start.14 = (bf16[32,32,128]{2,1,0:T(8,128)(2,1)S(1)}, bf16[32,32,128]{2,1,0:T(8,128)(2,1)}, u32[]{:S(2)}) copy-start(bf16[32,32,128]{2,1,0:T(8,128)(2,1)} %get-tuple-element.33) | copy-start | bytes 786436
  104.3 1.0 copy-start.11
  104.4 1.3 copy-start.17
  104.7 1.3 copy-start.13
  105.6 1.1 copy-start.16
  106.0 1.1 copy-start.12
  106.4 1.1 copy-start.10
  106.7 1.1 copy-start.15
  108.1 1.0 copy-start.8
  112.4 193.9 %all-reduce.9.cloned.1.call-start = ((), (), s32[]{:S(2)}) async-start(), calls=%async_computation.3 | async-start | bytes 2359296 | tf_op jit(solution)/shard_map/psum | solution.py:167
  112.8 0.7 copy-start.40
  113.5 0.7 copy-start.21
  113.5 0.7 copy-start.23
  215.9 92.7 %copy-start.1 = (bf16[9,256,128]{2,1,0:T(8,128)(2,1)S(1)}, bf16[9,256,128]{2,1,0:T(8,128)(2,1)}, u32[]{:S(2)}) copy-start(bf16[9,256,128]{2,1,0:T(8,128)(2,1)} %param.11) | copy-start | bytes 1769476
Sparse Core Ops, SparseCore 0:
  112.5 95.9 all-gather.3
  212.5 93.6 all-reduce.8
